TPU v7x, 512 devices: a whole 4x4x16 slice. The times are simulated.
512 devices in a mesh: pairs: 128 (over x, z, core), ints: 4 (over y).
Axes of the slice: x: 4, y: 4, z: 16, core: 2. Of those that a mesh axis runs over, the one named last changes fastest.
Arguments:
- amps: float32 [256, 256, 256], P('pairs', 'ints'), may hold values from -0.8 to 0.8
- resid_rest: float32 [256, 256, 256], P('pairs', 'ints'), may hold values from -6 to 6
- int_blocks: bfloat16 [128, 256, 256], P('pairs'), may hold values from -0.375 to 0.375
- virt_energy: float32 [256, 256], P('pairs'), may hold values from 0.5 to 3
- pair_energy: float32 [256], P('pairs'), may hold values from -2 to -0.5
- item_block: int32 [32768, 1], P(('pairs', 'ints')), may hold values from 0 to 127; in each aligned block of 64 rows (0 to 63, 64 to 127, ...) at most 2 rows name the same one
- share_owner: int32 [12288, 1], P('pairs'), may hold values from 0 to 127; in each aligned block of 96 rows (0 to 95, 96 to 191, ...) at most 2 rows name the same one
- share_pair: int32 [12288, 1], P('pairs'), may hold values from 0 to 1
- share_amp: int32 [12288, 1], P('pairs'), may hold values from 0 to 1
- transpose_pair: int32 [256], P('pairs'), may hold values from 0 to 255, as said below
Outputs:
- update: float32 [256, 256, 256], P('pairs', 'ints')
Inputs may be any that keep to these rules, and one draw needn't show every extreme that they name: `item_block`: within each aligned block of 64 rows no value occurs more than 2 times, and some value occurs exactly 2 times. `share_owner`: within each aligned block of 96 rows no value occurs more than 2 times, and some value occurs exactly 2 times. `transpose_pair`: A permutation equal to its own inverse; pair p maps into the block of 2 consecutive pairs whose block number is (p // 2 + 256 // 4) modulo 256 // 2.
All inputs are finite; a program needn't handle non-finite values.
Results may differ from a plain program's by a relative error of at most 0.008.
Values may be sent and summed in bfloat16 or wider, within the bound.
A program may use at most 64 MiB of HBM per device.

v0:
```python
import jax
import jax.numpy as jnp
from jax import lax
from jax.sharding import Mesh
from jax.sharding import PartitionSpec as P

PAIRS = ("pairs_0", "pairs_1", "pairs_2")
PAIRS_INTS = ("pairs_0", "pairs_1", "pairs_2", "ints")


def in_blocks(array, dim, size):
    before, after = (array.shape[:dim], array.shape[dim + 1 :])
    return jnp.moveaxis(array.reshape(*before, size, -1, *after), dim, 0)


def sum_at_owner(array, axis, dim):
    tiles = in_blocks(array, dim, lax.axis_size(axis))
    arrived = lax.all_to_all(tiles, axis, split_axis=0, concat_axis=0, tiled=True)
    return arrived.astype(jnp.float32).sum(axis=0)


def laid_out(tiles, dim):
    dims = list(tiles.shape[1:])
    dims[dim] *= tiles.shape[0]
    return jnp.moveaxis(tiles, 0, dim).reshape(dims)


def stacked_from(array, axes, order):
    tiles = array
    for k in order:
        tiles = lax.all_gather(tiles, axes[k])
    done = order[::-1]
    back = [done.index(k) for k in range(len(axes))]
    tiles = tiles.transpose(*back, *range(len(axes), tiles.ndim))
    return tiles.reshape(-1, *array.shape)


def gather_axes(array, axes, order, dim):
    return laid_out(stacked_from(array, axes, order), dim)


def from_behind(value, axis, steps):
    count = lax.axis_size(axis)
    pairs = [(source, (source + steps) % count) for source in range(count)]
    return lax.ppermute(value, axis, pairs)


def slot_ranks(targets, n_groups):
    match_hits = (targets[:, None] == jnp.arange(n_groups, dtype=jnp.int32)[None, :]).astype(
        jnp.int32
    )
    before = jnp.cumsum(match_hits, axis=0) - match_hits
    return jnp.sum(before * match_hits, axis=1)


def body(
    amps,
    resid_rest,
    int_blocks,
    virt_energy,
    pair_energy,
    item_block,
    share_owner,
    share_pair,
    share_amp,
    transpose_pair,
):
    n_pairs = lax.axis_size(PAIRS)
    pair_index = lax.axis_index(PAIRS)
    quarter = lax.axis_index("ints")
    pair_count, row_count, domain = amps.shape
    amp_half = amps.astype(jnp.bfloat16)
    n_items = item_block.shape[0]
    item_height = pair_count * row_count // n_items
    item_rows = amp_half.reshape(n_items, item_height, domain)
    block_targets = item_block[:, 0]
    cap_items = max(2, 3 * n_items // (2 * n_pairs))
    item_slot = block_targets * cap_items + slot_ranks(block_targets, n_pairs)
    outgoing = (
        jnp.zeros((n_pairs * cap_items, item_height, domain), jnp.bfloat16)
        .at[item_slot]
        .set(item_rows)
    )
    outgoing = outgoing.reshape(n_pairs, cap_items, item_height, domain)
    resident = int_blocks[0]
    arrived = lax.all_to_all(outgoing, PAIRS, split_axis=0, concat_axis=0, tiled=True)
    leading = arrived.shape[:3]
    product = jnp.dot(arrived.reshape(-1, domain), resident, preferred_element_type=jnp.float32)
    product = product.astype(jnp.bfloat16).reshape(leading + (domain,))
    returned = lax.all_to_all(product, PAIRS, split_axis=0, concat_axis=0, tiled=True)
    x_rows = returned.reshape(n_pairs * cap_items, item_height, domain)[item_slot]
    x_rows = x_rows.reshape(pair_count, row_count, domain)
    partial_value = jnp.einsum("pac,pad->pcd", amp_half, x_rows, preferred_element_type=jnp.float32)
    intermed = sum_at_owner(partial_value.astype(jnp.bfloat16), "ints", 1).astype(jnp.bfloat16)
    amp_full = lax.all_gather(amp_half, "ints", axis=1, tiled=True)
    owners = share_owner[:, 0]
    wanted = share_pair[:, 0]
    n_req = owners.shape[0]
    per_pair = n_req // pair_count
    source_global = owners * pair_count + wanted
    empty_rows = jnp.zeros((n_req, row_count, domain), jnp.bfloat16)
    piece = gather_axes(intermed, PAIRS, (0, 1, 2), 0)
    start = jnp.int32(0)
    local = jnp.clip(source_global, 0, piece.shape[0] - 1)
    inside = (source_global >= start) & (source_global < start + piece.shape[0])
    picked = jnp.where(inside[:, None, None], piece[local], empty_rows)
    picked = picked.reshape(pair_count, per_pair, row_count, domain)
    partners = share_amp[:, 0].reshape(pair_count, per_pair)

    def cycle_one(packed):
        w_req, amp_index = packed
        return jnp.einsum(
            "kac,kcb->ab", w_req, amp_full[amp_index], preferred_element_type=jnp.float32
        )

    cycle_term = lax.map(cycle_one, (picked, partners))
    energies_rows = lax.dynamic_slice_in_dim(virt_energy, quarter * row_count, row_count, 1)
    divisor = energies_rows[:, :, None] + virt_energy[:, None, :] - pair_energy[:, None, None]
    scaled = (resid_rest + cycle_term) / divisor
    mirror_part = from_behind(scaled.astype(jnp.bfloat16), PAIRS, n_pairs // 2).astype(scaled.dtype)
    turned = lax.all_to_all(
        mirror_part.astype(jnp.bfloat16), "ints", split_axis=2, concat_axis=1, tiled=True
    ).astype(mirror_part.dtype)
    partner_dev = (pair_index + n_pairs // 2) % n_pairs
    local_swap = transpose_pair - partner_dev * pair_count
    mirrored = jnp.transpose(turned[local_swap], (0, 2, 1))
    return -0.5 * (scaled + mirrored)


def solution(mesh):
    torus = Mesh(
        mesh.devices.reshape(4, 16, 2, mesh.shape["ints"]),
        ("pairs_0", "pairs_1", "pairs_2", "ints"),
    )
    return jax.shard_map(
        body,
        mesh=torus,
        in_specs=(
            P(PAIRS, "ints", None),
            P(PAIRS, "ints", None),
            P(PAIRS, None, None),
            P(PAIRS, None),
            P(PAIRS),
            P(PAIRS_INTS, None),
            P(PAIRS, None),
            P(PAIRS, None),
            P(PAIRS, None),
            P(PAIRS),
        ),
        out_specs=P(PAIRS, "ints", None),
        check_vma=False,
    )
```

profile of v0, /device:TPU:2, one launch (start us, length us, event | category | flops | bytes accessed | tf_op | source)
XLA Modules:
  0.0 273.0 jit_solution(6148034309779576829)
XLA Ops:
  8.9 0.9 convert_element_type.35
  10.0 2.4 scatter_fusion
  12.4 42.1 %all_to_all.24 = bf16[128,2,2,256]{3,2,1,0:T(2,128)(2,1)S(1)} all-to-all(bf16[128,2,2,256]{3,2,1,0:T(2,128)(2,1)S(1)} %bitcast.79), channel_id=1, replica_groups=mesh['pairs_0'=4,'pairs_1'=16,'pairs_2'=2,'ints'=4] {'pairs_0','pairs_1'..., dimensions={0} | all-to-all | bytes 524288 | tf_op jit(solution)/shard_map/all_to_all | solution.py:86
  55.6 7.1 %all-to-all-start.1 = ((bf16[128,2,2,256]{3,2,1,0:T(2,128)(2,1)}), bf16[128,2,2,256]{3,2,1,0:T(2,128)(2,1)S(1)}, u32[]{:S(2)}, u32[]{:S(2)}) async-start(bf16[128,2,2,256]{3,2,1,0:T(2,128)(2,1)} %reshape.85), calls=%async_computation.1 | async-start | bytes 524288 | tf_op jit(solution)/shard_map/all_to_all | solution.py:90
  62.8 22.7 %all-to-all-done.1 = bf16[128,2,2,256]{3,2,1,0:T(2,128)(2,1)S(1)} async-done(((bf16[128,2,2,256]{3,2,1,0:T(2,128)(2,1)}), bf16[128,2,2,256]{3,2,1,0:T(2,128)(2,1)S(1)}, u32[]{:S(2)}, u32[]{:S(2)}) %all-to-all-start.1) | async-done | bytes 262176 | tf_op jit(solution)/shard_map/all_to_all | solution.py:90
  86.6 11.0 %all_to_all.25 = bf16[4,2,64,256]{3,2,1,0:T(8,128)(2,1)S(1)} all-to-all(bf16[4,2,64,256]{3,2,1,0:T(8,128)(2,1)S(1)} %bitcast.83), channel_id=1, replica_groups=mesh['pairs_0'=4,'pairs_1'=16,'pairs_2'=2,'ints'=4] {'ints'}, dimensions={0} | all-to-all | bytes 524288 | tf_op jit(solution)/shard_map/all_to_all | solution.py:18
  97.6 12.2 %all-gather = bf16[8,64,256]{2,1,0:T(8,128)(2,1)} all-gather(bf16[2,64,256]{2,1,0:T(8,128)(2,1)S(1)} %reduce_sum.25), channel_id=2, replica_groups=mesh['pairs_0'=4,'pairs_1'=16,'pairs_2'=2,'ints'=4] {'pairs_0'}, dimensions={0}, use_global_device_ids=true | all-gather | bytes 327680 | tf_op jit(solution)/shard_map/all_gather | solution.py:31
  109.9 68.5 %all-gather.6.cloned.1.call-done = bf16[64,2,64,256]{3,2,1,0:T(8,128)(2,1)} async-done(((bf16[4,2,64,256]{3,2,1,0:T(8,128)(2,1)}), bf16[64,2,64,256]{3,2,1,0:T(8,128)(2,1)}) %all-gather.6.cloned.1.call-update) | async-done | bytes 4194320 | tf_op jit(solution)/shard_map/all_gather | solution.py:31
  180.4 12.6 %all_gather.27 = bf16[2,256,256]{2,1,0:T(8,128)(2,1)S(1)} all-gather(bf16[2,64,256]{2,1,0:T(8,128)(2,1)S(1)} %convert_element_type.35), channel_id=1, replica_groups=mesh['pairs_0'=4,'pairs_1'=16,'pairs_2'=2,'ints'=4] {'ints'}, dimensions={1}, use_global_device_ids=true | all-gather | bytes 327680 | tf_op jit(solution)/shard_map/all_gather | solution.py:95
  193.0 14.2 %all-gather.8.cloned.1.call-done = bf16[32,4,2,64,256]{4,3,2,1,0:T(8,128)(2,1)} async-done(((bf16[16,4,2,64,256]{4,3,2,1,0:T(8,128)(2,1)}), bf16[32,4,2,64,256]{4,3,2,1,0:T(8,128)(2,1)}) %all-gather.8.cloned.1.call-update) | async-done | bytes 8388624 | tf_op jit(solution)/shard_map/all_gather | solution.py:31
  207.2 8.3 %copy.15 = bf16[4,16,2,2,64,256]{5,4,3,2,1,0:T(8,128)(2,1)} copy(bf16[4,16,2,2,64,256]{5,4,3,0,1,2:T(8,128)(2,1)} %bitcast.77) | data formatting | bytes 16777216 | tf_op jit(solution)/shard_map/transpose | solution.py:34
  215.4 5.9 %gather_fusion.2 = bf16[96,64,256]{2,1,0:T(8,128)(2,1)} fusion(bf16[256,64,256]{2,1,0:T(8,128)(2,1)} %bitcast.75, s32[1024]{0:T(1024)S(1)} %pad_clamp_fusion.2), kind=kCustom, calls=%fused_computation.2 | custom fusion | bytes 6291840 | tf_op jit(solution)/shard_map/gather | solution.py:106
  221.4 2.2 broadcast_select_fusion
  223.6 20.3 %while.10 = (s32[]{:T(128)}, f32[2,64,256]{2,1,0:T(8,128)}, bf16[2,48,64,256]{3,2,1,0:T(8,128)(2,1)S(1)}, s32[2,48]{1,0:T(2,128)}, bf16[2,256,256]{2,1,0:T(8,128)(2,1)S(1)}, /*index=5*/s32[]{:T(128)}) while((s32[]{:T(128)}, f32[2,64,256]{2,1,0:T(8,128)}, bf16[2,48,64,256]{3,2,1,0:T(8,128)(2,1)S(1)}, s32[2,48]{1,0:T(2,128)}, ...), condition=%wide.region_5.6_spmd, body=%wide.region_4.5_spmd.sunk | while | flops 402654368 | bytes 20518728 | solution.py:116
  224.2 4.9 %gather_fusion = bf16[48,256,256]{2,1,0:T(8,128)(2,1)} fusion(bf16[2,256,256]{2,1,0:T(8,128)(2,1)S(1)} %get-tuple-element.90, s32[1024]{0:T(1024)S(1)} %pad_clamp_fusion.5), kind=kCustom, calls=%fused_computation.clone.1 | custom fusion | bytes 12583104 | tf_op jit(solution)/shard_map/while/body/eval_jaxpr/gather | solution.py:113
  229.1 4.6 %fusion.29 = f32[2,64,256]{2,1,0:T(8,128)} fusion(f32[2,64,256]{2,1,0:T(8,128)} %get-tuple-element.81, s32[]{:T(128)} %get-tuple-element.80, bf16[48,256,256]{2,1,0:T(8,128)(2,1)} %gather_fusion, bf16[2,48,64,256]{3,2,1,0:T(8,128)(2,1)S(1)} %get-tuple-element.88), kind=kOutput, calls=%fused_computation.9.clone.1 | convolution fusion | flops 402653184 | bytes 7930880 | tf_op jit(solution)/shard_map/while/body/eval_jaxpr/kac,kcb->ab/dot_general | solution.py:112
  234.4 4.8 %gather_fusion = bf16[48,256,256]{2,1,0:T(8,128)(2,1)} fusion(bf16[2,256,256]{2,1,0:T(8,128)(2,1)S(1)} %get-tuple-element.90, s32[1024]{0:T(1024)S(1)} %pad_clamp_fusion.5), kind=kCustom, calls=%fused_computation.clone.1 | custom fusion | bytes 12583104 | tf_op jit(solution)/shard_map/while/body/eval_jaxpr/gather | solution.py:113
  239.2 4.6 %fusion.29 = f32[2,64,256]{2,1,0:T(8,128)} fusion(f32[2,64,256]{2,1,0:T(8,128)} %get-tuple-element.81, s32[]{:T(128)} %get-tuple-element.80, bf16[48,256,256]{2,1,0:T(8,128)(2,1)} %gather_fusion, bf16[2,48,64,256]{3,2,1,0:T(8,128)(2,1)S(1)} %get-tuple-element.88), kind=kOutput, calls=%fused_computation.9.clone.1 | convolution fusion | flops 402653184 | bytes 7930880 | tf_op jit(solution)/shard_map/while/body/eval_jaxpr/kac,kcb->ab/dot_general | solution.py:112
  243.8 1.1 fusion.17
  244.9 3.9 %collective-permute-start = (bf16[2,64,256]{2,1,0:T(8,128)(2,1)S(1)}, bf16[2,64,256]{2,1,0:T(8,128)(2,1)S(1)}, u32[]{:S(2)}, u32[]{:S(2)}) collective-permute-start(bf16[2,64,256]{2,1,0:T(8,128)(2,1)S(1)} %fusion.17), channel_id=1, source_target_pairs={{0,256},{4,260},{8,264},{12,268},{16,272},{20,276},{24,280},{28,28... | collective-permute-start | bytes 196616 | tf_op jit(solution)/shard_map/ppermute | solution.py:45
  249.5 3.1 %collective-permute-done = bf16[2,64,256]{2,1,0:T(8,128)(2,1)S(1)} collective-permute-done((bf16[2,64,256]{2,1,0:T(8,128)(2,1)S(1)}, bf16[2,64,256]{2,1,0:T(8,128)(2,1)S(1)}, u32[]{:S(2)}, u32[]{:S(2)}) %collective-permute-start) | collective-permute-done | bytes 65568 | tf_op jit(solution)/shard_map/ppermute | solution.py:45
  253.5 4.3 %all-to-all-start.3 = ((bf16[4,2,4096]{2,1,0:T(2,128)(2,1)}), bf16[4,2,4096]{2,1,0:T(2,128)(2,1)S(1)}, u32[]{:S(2)}, u32[]{:S(2)}) async-start(bf16[4,2,4096]{2,1,0:T(2,128)(2,1)} %reshape.152), calls=%async_computation.3 | async-start | bytes 131072 | tf_op jit(solution)/shard_map/all_to_all | solution.py:121
  257.8 5.6 %all-to-all-done.3 = bf16[4,2,4096]{2,1,0:T(2,128)(2,1)S(1)} async-done(((bf16[4,2,4096]{2,1,0:T(2,128)(2,1)}), bf16[4,2,4096]{2,1,0:T(2,128)(2,1)S(1)}, u32[]{:S(2)}, u32[]{:S(2)}) %all-to-all-start.3) | async-done | bytes 65568 | tf_op jit(solution)/shard_map/all_to_all | solution.py:121
  264.4 1.7 fusion.12
  (52 shorter events, 10.8 us)
Async XLA Ops:
  6.5 48.1 %copy-start = (bf16[1,256,256]{2,1,0:T(8,128)(2,1)S(1)}, bf16[1,256,256]{2,1,0:T(8,128)(2,1)}, u32[]{:S(2)}) copy-start(bf16[1,256,256]{2,1,0:T(8,128)(2,1)} %param.14) | copy-start | bytes 393220
  55.6 29.9 %all-to-all-start.1 = ((bf16[128,2,2,256]{3,2,1,0:T(2,128)(2,1)}), bf16[128,2,2,256]{3,2,1,0:T(2,128)(2,1)S(1)}, u32[]{:S(2)}, u32[]{:S(2)}) async-start(bf16[128,2,2,256]{3,2,1,0:T(2,128)(2,1)} %reshape.85), calls=%async_computation.1 | async-start | bytes 524288 | tf_op jit(solution)/shard_map/all_to_all | solution.py:90
  62.8 115.5 %all-gather.6.cloned.1.call-start = ((), (), s32[]{:S(2)}) async-start(), calls=%async_computation.4 | async-start | bytes 4456448 | tf_op jit(solution)/shard_map/all_gather | solution.py:31
  86.5 91.8 %copy-start.4 = (s32[96,1]{0,1:T(1,128)S(1)}, s32[96,1]{0,1:T(1,128)}, u32[]{:S(2)}) copy-start(s32[96,1]{0,1:T(1,128)} %param.19) | copy-start | bytes 1156
  86.5 91.8 %copy-start.5 = (s32[96,1]{0,1:T(1,128)S(1)}, s32[96,1]{0,1:T(1,128)}, u32[]{:S(2)}) copy-start(s32[96,1]{0,1:T(1,128)} %param.18) | copy-start | bytes 1156
  86.6 92.5 %copy-start.3 = (s32[96,1]{0,1:T(1,128)S(1)}, s32[96,1]{0,1:T(1,128)}, u32[]{:S(2)}) copy-start(s32[96,1]{0,1:T(1,128)} %param.20) | copy-start | bytes 1156
  86.6 106.3 %copy-start.1 = (f32[2,256]{1,0:T(2,128)S(1)}, f32[2,256]{1,0:T(2,128)}, u32[]{:S(2)}) copy-start(f32[2,256]{1,0:T(2,128)} %param.15) | copy-start | bytes 6148
  109.8 97.4 %all-gather.8.cloned.1.call-start = ((), (), s32[]{:S(2)}) async-start(), calls=%async_computation.5 | async-start | bytes 12582912 | tf_op jit(solution)/shard_map/all_gather | solution.py:31
  223.6 20.3 %copy-start.2 = (f32[2]{0:T(128)S(1)}, f32[2]{0:T(128)}, u32[]{:S(2)}) copy-start(f32[2]{0:T(128)} %param.16) | copy-start | bytes 28
  244.9 7.7 %collective-permute-start = (bf16[2,64,256]{2,1,0:T(8,128)(2,1)S(1)}, bf16[2,64,256]{2,1,0:T(8,128)(2,1)S(1)}, u32[]{:S(2)}, u32[]{:S(2)}) collective-permute-start(bf16[2,64,256]{2,1,0:T(8,128)(2,1)S(1)} %fusion.17), channel_id=1, source_target_pairs={{0,256},{4,260},{8,264},{12,268},{16,272},{20,276},{24,280},{28,28... | collective-permute-start | bytes 196616 | tf_op jit(solution)/shard_map/ppermute | solution.py:45
  253.5 9.9 %all-to-all-start.3 = ((bf16[4,2,4096]{2,1,0:T(2,128)(2,1)}), bf16[4,2,4096]{2,1,0:T(2,128)(2,1)S(1)}, u32[]{:S(2)}, u32[]{:S(2)}) async-start(bf16[4,2,4096]{2,1,0:T(2,128)(2,1)} %reshape.152), calls=%async_computation.3 | async-start | bytes 131072 | tf_op jit(solution)/shard_map/all_to_all | solution.py:121
Sparse Core Ops, SparseCore 0:
  109.9 68.3 all-gather.5
  180.4 26.7 all-gather.7
where the time goes:
time: 274 us; the launch traced here: 273 us
  waiting for transfers between devices  114 us (42%)
  blocking collectives  77.8 us (28%)
  local copies, waits for them, and re-layouts  31.5 us (11%)
  starting transfers between devices  15.4 us (6%)
  between operations  13.6 us (5%)
  other arithmetic  11 us (4%)
  matrix products  9.71 us (4%)
    all_gather x2, waiting for transfers between devices, stacked_from(): tiles = lax.all_gather(tiles, axes[k])  82.6 us
    all_to_all x1, blocking collectives, body(): lax.all_to_all(outgoing, PAIRS, split_axis=0, concat_axis=0, tiled=True)  42.1 us
    all_to_all x1, waiting for transfers between devices, body(): lax.all_to_all(product, PAIRS, split_axis=0, concat_axis=0, tiled=True)  22.7 us
    all_gather x1, blocking collectives, body(): amp_full = lax.all_gather(amp_half, 'ints', axis=1, tiled=True)  12.6 us
    all_gather x1, blocking collectives, stacked_from(): tiles = lax.all_gather(tiles, axes[k])  12.2 us
    all_to_all x1, blocking collectives, sum_at_owner(): lax.all_to_all(tiles, axis, split_axis=0, concat_axis=0, tiled=True)  11 us
    gather x2, local copies, waits for them, and re-layouts, cycle_one(): amp_full[amp_index]  9.71 us
    dot_general x2, matrix products, cycle_one(): jnp.einsum('kac,kcb->ab', w_req, amp_full[amp_index], preferred_element_t...  9.23 us
  transfers between devices with their start and end apart: 5, of which 5 were waited for; matrix products, arithmetic and copies ran while one was open for 1% of the time, Pallas kernels for 0%

commit v1 on v0

--- a/solution.py
+++ b/solution.py
@@ -92,7 +92,9 @@
     x_rows = x_rows.reshape(pair_count, row_count, domain)
     partial_value = jnp.einsum("pac,pad->pcd", amp_half, x_rows, preferred_element_type=jnp.float32)
     intermed = sum_at_owner(partial_value.astype(jnp.bfloat16), "ints", 1).astype(jnp.bfloat16)
-    amp_full = lax.all_gather(amp_half, "ints", axis=1, tiled=True)
+    amp_full = jnp.concatenate(
+        lax.all_to_all(jnp.stack([amp_half] * lax.axis_size("ints")), "ints", 0, 0), axis=1
+    )
     owners = share_owner[:, 0]
     wanted = share_pair[:, 0]
     n_req = owners.shape[0]

time: 274 us -> 274 us (level)
  blocking collectives: 77.8 us -> 65.2 us
  waiting for transfers between devices: 114 us -> 122 us
  starting transfers between devices: 15.4 us -> 19.6 us
    all_gather x1 -> x0, blocking collectives: 12.6 us -> none  [body(): amp_full = lax.all_gather(amp_half, 'ints', axis=1, tiled=True)]
    all_to_all x0 -> x1, waiting for transfers between devices: none -> 4.51 us  [body(): lax.all_to_all(jnp.stack([amp_half] * lax.axis_size('ints')), 'ints', 0, 0)]
    all_to_all x0 -> x1, starting transfers between devices: none -> 4.28 us  [body(): lax.all_to_all(jnp.stack([amp_half] * lax.axis_size('ints')), 'ints', 0, 0)]
    all_gather x2, waiting for transfers between devices: 82.6 us -> 85.6 us  [stacked_from(): tiles = lax.all_gather(tiles, axes[k])]
  transfers between devices with their start and end apart: 5 -> 6, of which waited for: 5 -> 6; matrix products, arithmetic and copies ran while one was open for 1% -> 1% of each run, Pallas kernels for 0% -> 0%
where the time goes in v1:
time: 274 us; the launch traced here: 273 us
  waiting for transfers between devices  122 us (45%)
  blocking collectives  65.2 us (24%)
  local copies, waits for them, and re-layouts  32.2 us (12%)
  starting transfers between devices  19.6 us (7%)
  between operations  13.6 us (5%)
  other arithmetic  11.1 us (4%)
  matrix products  9.72 us (4%)
    all_gather x2, waiting for transfers between devices, stacked_from(): tiles = lax.all_gather(tiles, axes[k])  85.6 us
    all_to_all x1, blocking collectives, body(): lax.all_to_all(outgoing, PAIRS, split_axis=0, concat_axis=0, tiled=True)  42.1 us
    all_to_all x1, waiting for transfers between devices, body(): lax.all_to_all(product, PAIRS, split_axis=0, concat_axis=0, tiled=True)  22.7 us
    all_gather x1, blocking collectives, stacked_from(): tiles = lax.all_gather(tiles, axes[k])  12.2 us
    all_to_all x1, blocking collectives, sum_at_owner(): lax.all_to_all(tiles, axis, split_axis=0, concat_axis=0, tiled=True)  11 us
    gather x2, local copies, waits for them, and re-layouts, cycle_one(): amp_full[amp_index]  9.69 us
    dot_general x2, matrix products, cycle_one(): jnp.einsum('kac,kcb->ab', w_req, amp_full[amp_index], preferred_element_t...  9.23 us
    transpose x1, local copies, waits for them, and re-layouts, stacked_from(): tiles = tiles.transpose(*back, *range(len(axes), tiles.ndim))  8.27 us
  transfers between devices with their start and end apart: 6, of which 6 were waited for; matrix products, arithmetic and copies ran while one was open for 1% of the time, Pallas kernels for 0%

profile of v1, /device:TPU:2, one launch (start us, length us, event | category | flops | bytes accessed | tf_op | source)
XLA Modules:
  0.0 273.0 jit_solution(12679372218641172761)
XLA Ops:
  10.0 2.4 scatter_fusion
  12.4 42.1 %all_to_all.29 = bf16[128,2,2,256]{3,2,1,0:T(2,128)(2,1)S(1)} all-to-all(bf16[128,2,2,256]{3,2,1,0:T(2,128)(2,1)S(1)} %bitcast.83), channel_id=1, replica_groups=mesh['pairs_0'=4,'pairs_1'=16,'pairs_2'=2,'ints'=4] {'pairs_0','pairs_1'..., dimensions={0} | all-to-all | bytes 524288 | tf_op jit(solution)/shard_map/all_to_all | solution.py:86
  55.6 7.1 %all-to-all-start.1 = ((bf16[128,2,2,256]{3,2,1,0:T(2,128)(2,1)}), bf16[128,2,2,256]{3,2,1,0:T(2,128)(2,1)S(1)}, u32[]{:S(2)}, u32[]{:S(2)}) async-start(bf16[128,2,2,256]{3,2,1,0:T(2,128)(2,1)} %reshape.93), calls=%async_computation.1 | async-start | bytes 524288 | tf_op jit(solution)/shard_map/all_to_all | solution.py:90
  62.8 22.7 %all-to-all-done.1 = bf16[128,2,2,256]{3,2,1,0:T(2,128)(2,1)S(1)} async-done(((bf16[128,2,2,256]{3,2,1,0:T(2,128)(2,1)}), bf16[128,2,2,256]{3,2,1,0:T(2,128)(2,1)S(1)}, u32[]{:S(2)}, u32[]{:S(2)}) %all-to-all-start.1) | async-done | bytes 262176 | tf_op jit(solution)/shard_map/all_to_all | solution.py:90
  86.6 11.0 %all_to_all.30 = bf16[4,2,64,256]{3,2,1,0:T(8,128)(2,1)S(1)} all-to-all(bf16[4,2,64,256]{3,2,1,0:T(8,128)(2,1)S(1)} %bitcast.87), channel_id=1, replica_groups=mesh['pairs_0'=4,'pairs_1'=16,'pairs_2'=2,'ints'=4] {'ints'}, dimensions={0} | all-to-all | bytes 524288 | tf_op jit(solution)/shard_map/all_to_all | solution.py:18
  97.6 12.2 %all-gather = bf16[8,64,256]{2,1,0:T(8,128)(2,1)} all-gather(bf16[2,64,256]{2,1,0:T(8,128)(2,1)S(1)} %reduce_sum.25), channel_id=2, replica_groups=mesh['pairs_0'=4,'pairs_1'=16,'pairs_2'=2,'ints'=4] {'pairs_0'}, dimensions={0}, use_global_device_ids=true | all-gather | bytes 327680 | tf_op jit(solution)/shard_map/all_gather | solution.py:31
  109.8 68.5 %all-gather.6.cloned.1.call-done = bf16[64,2,64,256]{3,2,1,0:T(8,128)(2,1)} async-done(((bf16[4,2,64,256]{3,2,1,0:T(8,128)(2,1)}), bf16[64,2,64,256]{3,2,1,0:T(8,128)(2,1)}) %all-gather.6.cloned.1.call-update) | async-done | bytes 4194320 | tf_op jit(solution)/shard_map/all_gather | solution.py:31
  179.0 4.3 %all-to-all-start.3 = ((bf16[4,2,64,256]{3,2,1,0:T(8,128)(2,1)}), bf16[4,2,64,256]{3,2,1,0:T(8,128)(2,1)S(1)}, u32[]{:S(2)}, u32[]{:S(2)}) async-start(bf16[4,2,64,256]{3,2,1,0:T(8,128)(2,1)} %stack.2), calls=%async_computation.3 | async-start | bytes 524288 | tf_op jit(solution)/shard_map/all_to_all | solution.py:96
  185.5 4.5 %all-to-all-done.3 = bf16[4,2,64,256]{3,2,1,0:T(8,128)(2,1)S(1)} async-done(((bf16[4,2,64,256]{3,2,1,0:T(8,128)(2,1)}), bf16[4,2,64,256]{3,2,1,0:T(8,128)(2,1)S(1)}, u32[]{:S(2)}, u32[]{:S(2)}) %all-to-all-start.3) | async-done | bytes 262176 | tf_op jit(solution)/shard_map/all_to_all | solution.py:96
  190.0 17.1 %all-gather.8.cloned.1.call-done = bf16[32,4,2,64,256]{4,3,2,1,0:T(8,128)(2,1)} async-done(((bf16[16,4,2,64,256]{4,3,2,1,0:T(8,128)(2,1)}), bf16[32,4,2,64,256]{4,3,2,1,0:T(8,128)(2,1)}) %all-gather.8.cloned.1.call-update) | async-done | bytes 8388624 | tf_op jit(solution)/shard_map/all_gather | solution.py:31
  207.2 8.3 %copy.19 = bf16[4,16,2,2,64,256]{5,4,3,2,1,0:T(8,128)(2,1)} copy(bf16[4,16,2,2,64,256]{5,4,3,0,1,2:T(8,128)(2,1)} %bitcast.81) | data formatting | bytes 16777216 | tf_op jit(solution)/shard_map/transpose | solution.py:34
  215.4 5.9 %gather_fusion.2 = bf16[96,64,256]{2,1,0:T(8,128)(2,1)} fusion(bf16[256,64,256]{2,1,0:T(8,128)(2,1)} %bitcast.79, s32[1024]{0:T(1024)S(1)} %pad_clamp_fusion.2), kind=kCustom, calls=%fused_computation.2 | custom fusion | bytes 6291840 | tf_op jit(solution)/shard_map/gather | solution.py:108
  221.3 2.2 broadcast_select_fusion
  223.5 20.3 %while.10 = (s32[]{:T(128)}, f32[2,64,256]{2,1,0:T(8,128)}, bf16[2,48,64,256]{3,2,1,0:T(8,128)(2,1)S(1)}, s32[2,48]{1,0:T(2,128)}, bf16[2,256,256]{2,1,0:T(8,128)(2,1)S(1)}, /*index=5*/s32[]{:T(128)}) while((s32[]{:T(128)}, f32[2,64,256]{2,1,0:T(8,128)}, bf16[2,48,64,256]{3,2,1,0:T(8,128)(2,1)S(1)}, s32[2,48]{1,0:T(2,128)}, ...), condition=%wide.region_5.6_spmd, body=%wide.region_4.5_spmd.sunk | while | flops 402654368 | bytes 20518728 | solution.py:118
  224.2 4.9 %gather_fusion = bf16[48,256,256]{2,1,0:T(8,128)(2,1)} fusion(bf16[2,256,256]{2,1,0:T(8,128)(2,1)S(1)} %get-tuple-element.90, s32[1024]{0:T(1024)S(1)} %pad_clamp_fusion.5), kind=kCustom, calls=%fused_computation.clone.1 | custom fusion | bytes 12583104 | tf_op jit(solution)/shard_map/while/body/eval_jaxpr/gather | solution.py:115
  229.1 4.6 %fusion.29 = f32[2,64,256]{2,1,0:T(8,128)} fusion(f32[2,64,256]{2,1,0:T(8,128)} %get-tuple-element.81, s32[]{:T(128)} %get-tuple-element.80, bf16[48,256,256]{2,1,0:T(8,128)(2,1)} %gather_fusion, bf16[2,48,64,256]{3,2,1,0:T(8,128)(2,1)S(1)} %get-tuple-element.88), kind=kOutput, calls=%fused_computation.9.clone.1 | convolution fusion | flops 402653184 | bytes 7930880 | tf_op jit(solution)/shard_map/while/body/eval_jaxpr/kac,kcb->ab/dot_general | solution.py:114
  234.4 4.8 %gather_fusion = bf16[48,256,256]{2,1,0:T(8,128)(2,1)} fusion(bf16[2,256,256]{2,1,0:T(8,128)(2,1)S(1)} %get-tuple-element.90, s32[1024]{0:T(1024)S(1)} %pad_clamp_fusion.5), kind=kCustom, calls=%fused_computation.clone.1 | custom fusion | bytes 12583104 | tf_op jit(solution)/shard_map/while/body/eval_jaxpr/gather | solution.py:115
  239.2 4.6 %fusion.29 = f32[2,64,256]{2,1,0:T(8,128)} fusion(f32[2,64,256]{2,1,0:T(8,128)} %get-tuple-element.81, s32[]{:T(128)} %get-tuple-element.80, bf16[48,256,256]{2,1,0:T(8,128)(2,1)} %gather_fusion, bf16[2,48,64,256]{3,2,1,0:T(8,128)(2,1)S(1)} %get-tuple-element.88), kind=kOutput, calls=%fused_computation.9.clone.1 | convolution fusion | flops 402653184 | bytes 7930880 | tf_op jit(solution)/shard_map/while/body/eval_jaxpr/kac,kcb->ab/dot_general | solution.py:114
  243.8 1.1 fusion.17
  244.9 3.9 %collective-permute-start = (bf16[2,64,256]{2,1,0:T(8,128)(2,1)S(1)}, bf16[2,64,256]{2,1,0:T(8,128)(2,1)S(1)}, u32[]{:S(2)}, u32[]{:S(2)}) collective-permute-start(bf16[2,64,256]{2,1,0:T(8,128)(2,1)S(1)} %fusion.17), channel_id=1, source_target_pairs={{0,256},{4,260},{8,264},{12,268},{16,272},{20,276},{24,280},{28,28... | collective-permute-start | bytes 196616 | tf_op jit(solution)/shard_map/ppermute | solution.py:45
  249.4 3.1 %collective-permute-done = bf16[2,64,256]{2,1,0:T(8,128)(2,1)S(1)} collective-permute-done((bf16[2,64,256]{2,1,0:T(8,128)(2,1)S(1)}, bf16[2,64,256]{2,1,0:T(8,128)(2,1)S(1)}, u32[]{:S(2)}, u32[]{:S(2)}) %collective-permute-start) | collective-permute-done | bytes 65568 | tf_op jit(solution)/shard_map/ppermute | solution.py:45
  253.5 4.3 %all-to-all-start.4 = ((bf16[4,2,4096]{2,1,0:T(2,128)(2,1)}), bf16[4,2,4096]{2,1,0:T(2,128)(2,1)S(1)}, u32[]{:S(2)}, u32[]{:S(2)}) async-start(bf16[4,2,4096]{2,1,0:T(2,128)(2,1)} %reshape.162), calls=%async_computation.4 | async-start | bytes 131072 | tf_op jit(solution)/shard_map/all_to_all | solution.py:123
  257.8 5.6 %all-to-all-done.4 = bf16[4,2,4096]{2,1,0:T(2,128)(2,1)S(1)} async-done(((bf16[4,2,4096]{2,1,0:T(2,128)(2,1)}), bf16[4,2,4096]{2,1,0:T(2,128)(2,1)S(1)}, u32[]{:S(2)}, u32[]{:S(2)}) %all-to-all-start.4) | async-done | bytes 65568 | tf_op jit(solution)/shard_map/all_to_all | solution.py:123
  264.4 1.7 fusion.12
  (55 shorter events, 12.6 us)
Async XLA Ops:
  6.5 48.1 %copy-start = (bf16[1,256,256]{2,1,0:T(8,128)(2,1)S(1)}, bf16[1,256,256]{2,1,0:T(8,128)(2,1)}, u32[]{:S(2)}) copy-start(bf16[1,256,256]{2,1,0:T(8,128)(2,1)} %param.14) | copy-start | bytes 393220
  55.6 29.9 %all-to-all-start.1 = ((bf16[128,2,2,256]{3,2,1,0:T(2,128)(2,1)}), bf16[128,2,2,256]{3,2,1,0:T(2,128)(2,1)S(1)}, u32[]{:S(2)}, u32[]{:S(2)}) async-start(bf16[128,2,2,256]{3,2,1,0:T(2,128)(2,1)} %reshape.93), calls=%async_computation.1 | async-start | bytes 524288 | tf_op jit(solution)/shard_map/all_to_all | solution.py:90
  62.8 115.5 %all-gather.6.cloned.1.call-start = ((), (), s32[]{:S(2)}) async-start(), calls=%async_computation.5 | async-start | bytes 4456448 | tf_op jit(solution)/shard_map/all_gather | solution.py:31
  97.5 85.8 %copy-start.4 = (s32[96,1]{0,1:T(1,128)S(1)}, s32[96,1]{0,1:T(1,128)}, u32[]{:S(2)}) copy-start(s32[96,1]{0,1:T(1,128)} %param.19) | copy-start | bytes 1156
  97.5 85.8 %copy-start.5 = (s32[96,1]{0,1:T(1,128)S(1)}, s32[96,1]{0,1:T(1,128)}, u32[]{:S(2)}) copy-start(s32[96,1]{0,1:T(1,128)} %param.18) | copy-start | bytes 1156
  97.5 86.5 %copy-start.3 = (s32[96,1]{0,1:T(1,128)S(1)}, s32[96,1]{0,1:T(1,128)}, u32[]{:S(2)}) copy-start(s32[96,1]{0,1:T(1,128)} %param.20) | copy-start | bytes 1156
  97.5 87.9 %copy-start.1 = (f32[2,256]{1,0:T(2,128)S(1)}, f32[2,256]{1,0:T(2,128)}, u32[]{:S(2)}) copy-start(f32[2,256]{1,0:T(2,128)} %param.15) | copy-start | bytes 6148
  109.8 97.4 %all-gather.8.cloned.1.call-start = ((), (), s32[]{:S(2)}) async-start(), calls=%async_computation.6 | async-start | bytes 12582912 | tf_op jit(solution)/shard_map/all_gather | solution.py:31
  179.0 11.0 %all-to-all-start.3 = ((bf16[4,2,64,256]{3,2,1,0:T(8,128)(2,1)}), bf16[4,2,64,256]{3,2,1,0:T(8,128)(2,1)S(1)}, u32[]{:S(2)}, u32[]{:S(2)}) async-start(bf16[4,2,64,256]{3,2,1,0:T(8,128)(2,1)} %stack.2), calls=%async_computation.3 | async-start | bytes 524288 | tf_op jit(solution)/shard_map/all_to_all | solution.py:96
  223.5 20.3 %copy-start.2 = (f32[2]{0:T(128)S(1)}, f32[2]{0:T(128)}, u32[]{:S(2)}) copy-start(f32[2]{0:T(128)} %param.16) | copy-start | bytes 28
  244.9 7.7 %collective-permute-start = (bf16[2,64,256]{2,1,0:T(8,128)(2,1)S(1)}, bf16[2,64,256]{2,1,0:T(8,128)(2,1)S(1)}, u32[]{:S(2)}, u32[]{:S(2)}) collective-permute-start(bf16[2,64,256]{2,1,0:T(8,128)(2,1)S(1)} %fusion.17), channel_id=1, source_target_pairs={{0,256},{4,260},{8,264},{12,268},{16,272},{20,276},{24,280},{28,28... | collective-permute-start | bytes 196616 | tf_op jit(solution)/shard_map/ppermute | solution.py:45
  253.5 9.9 %all-to-all-start.4 = ((bf16[4,2,4096]{2,1,0:T(2,128)(2,1)}), bf16[4,2,4096]{2,1,0:T(2,128)(2,1)S(1)}, u32[]{:S(2)}, u32[]{:S(2)}) async-start(bf16[4,2,4096]{2,1,0:T(2,128)(2,1)} %reshape.162), calls=%async_computation.4 | async-start | bytes 131072 | tf_op jit(solution)/shard_map/all_to_all | solution.py:123
Sparse Core Ops, SparseCore 0:
  109.9 68.3 all-gather.5
  180.4 26.7 all-gather.7
